TPU v7x, 32 devices: a whole 2x2x4 slice. The times are simulated.
32 devices in a mesh: seq: 4 (over z), tp: 4 (over y, x), fsdp: 2 (over core).
Axes of the slice: x: 2, y: 2, z: 4, core: 2. Of those that a mesh axis runs over, the one named last changes fastest.
Arguments:
- decoder_in: bfloat16 [32, 128, 1024], P(('seq', 'fsdp')), may hold values from -6 to 6
- memory: bfloat16 [32, 2048, 1024], P(('seq', 'fsdp')), may hold values from -6 to 6
- buckets: int32 [128, 128], replicated, may hold values from 0 to 31
- norm_gains: bfloat16 [3, 1024], P(None, ('seq', 'fsdp')), may hold values from 0.5 to 1.5
- rel_bias: bfloat16 [32, 16], P(('seq', 'fsdp'), 'tp'), may hold values from -4 to 4
- self_q: bfloat16 [1024, 1024], P(('seq', 'fsdp'), 'tp'), may hold values from -0.1875 to 0.1875
- self_kv: bfloat16 [1024, 2, 512], P(('seq', 'fsdp'), None, 'tp'), may hold values from -0.1875 to 0.1875
- self_out: bfloat16 [1024, 1024], P('tp', ('seq', 'fsdp')), may hold values from -0.75 to 0.75
- cross_q: bfloat16 [1024, 1024], P(('seq', 'fsdp'), 'tp'), may hold values from -0.1875 to 0.1875
- cross_kv: bfloat16 [1024, 2, 512], P(('seq', 'fsdp'), None, 'tp'), may hold values from -0.1875 to 0.1875
- cross_out: bfloat16 [1024, 1024], P('tp', ('seq', 'fsdp')), may hold values from -3 to 3
- gate_up: bfloat16 [1024, 2, 2816], P(('seq', 'fsdp'), None, 'tp'), may hold values from -0.1875 to 0.1875
- down: bfloat16 [2816, 1024], P('tp', ('seq', 'fsdp')), may hold values from -0.109375 to 0.109375
- cotangent: bfloat16 [32, 128, 1024], P(('seq', 'fsdp')), may hold values from -6 to 6
Outputs:
- decoder_out: bfloat16 [32, 128, 1024], P(('seq', 'fsdp'))
- decoder_grad: float32 [32, 128, 1024], P(('seq', 'fsdp'))
- memory_grad: bfloat16 [32, 2048, 1024], P(('seq', 'fsdp'), None, 'tp')
- gains_grad: float32 [3, 1024], P(None, ('seq', 'fsdp'))
- bias_grad: float32 [32, 16], P(('seq', 'fsdp'), 'tp')
- self_q_grad: float32 [1024, 1024], P(('seq', 'fsdp'), 'tp')
- self_kv_grad: float32 [1024, 2, 512], P(('seq', 'fsdp'), None, 'tp')
- self_out_grad: float32 [1024, 1024], P('tp', ('seq', 'fsdp'))
- cross_q_grad: float32 [1024, 1024], P(('seq', 'fsdp'), 'tp')
- cross_kv_grad: float32 [1024, 2, 512], P(('seq', 'fsdp'), None, 'tp')
- cross_out_grad: float32 [1024, 1024], P('tp', ('seq', 'fsdp'))
- gate_up_grad: float32 [1024, 2, 2816], P(('seq', 'fsdp'), None, 'tp')
- down_grad: float32 [2816, 1024], P('tp', ('seq', 'fsdp'))
Inputs may be any that keep to these rules, and one draw needn't show every extreme that they name: `buckets`: the bucket of query position i and key position j, the same for every sequence and head.
All inputs are finite; a program needn't handle non-finite values.
Results may differ from a plain program's by a relative error of at most 0.04.
Values may be sent and summed in bfloat16 or wider, within the bound.
No kernel may reach another device: no remote copies, remote signals or barrier semaphores. Data moves between devices by JAX's collectives and lax.ppermute only.
A program may use at most 192 MiB of HBM per device.

v0:
```python
import jax
import jax.numpy as jnp
from jax import lax
from jax.sharding import PartitionSpec as P

DH = 64
NB = 32
MICRO = 2


EPSILON = 1e-06
MASKED = -1e30


def rms_norm(values, gain):
    return values * lax.rsqrt(jnp.mean(values * values, axis=-1, keepdims=True) + EPSILON) * gain


def gelu_product(gate, up):
    return jax.nn.gelu(gate, approximate=True) * up


def flatten(weight):
    return weight.reshape(weight.shape[0], -1)


def gather_weights(
    gains, table, self_q, self_kv, self_out, cross_q, cross_kv, cross_out, gate_up, down
):
    return (
        lax.all_gather(gains, ("seq", "fsdp"), axis=1, tiled=True),
        lax.all_gather(table, ("seq", "fsdp"), axis=0, tiled=True),
        lax.all_gather(self_q, ("seq", "fsdp"), axis=0, tiled=True),
        lax.all_gather(self_kv, ("seq", "fsdp"), axis=0, tiled=True),
        lax.all_gather(self_out, ("seq", "fsdp"), axis=1, tiled=True),
        lax.all_gather(cross_q, ("seq", "fsdp"), axis=0, tiled=True),
        lax.all_gather(cross_kv, ("seq", "fsdp"), axis=0, tiled=True),
        lax.all_gather(cross_out, ("seq", "fsdp"), axis=1, tiled=True),
        lax.all_gather(gate_up, ("seq", "fsdp"), axis=0, tiled=True),
        lax.all_gather(down, ("seq", "fsdp"), axis=1, tiled=True),
    )


def branch_total(partial_value):
    return lax.psum(partial_value.astype(jnp.bfloat16), "tp").astype(jnp.float32)


def input_total(partial_value):
    return lax.psum(partial_value.astype(jnp.bfloat16), "tp").astype(jnp.float32)


def split_heads(query, keys, values):
    batch, rows, width = query.shape
    span = keys.shape[1]
    groups = keys.shape[2] // DH
    ratio = width // DH // groups
    return (
        query.reshape(batch, rows, groups, ratio, DH),
        keys.reshape(batch, span, groups, DH),
        values.reshape(batch, span, groups, DH),
    )


def scores_of(query_heads, key_heads, bias, causal):
    scores = jnp.einsum(
        "bigrd,bjgd->bgrij", query_heads, key_heads, preferred_element_type=jnp.float32
    ) * DH ** (-0.5)
    if bias is not None:
        scores = scores + bias
    if causal is not None:
        scores = jnp.where(causal, scores, MASKED)
    return scores


def attend_forward(query, keys, values, bias, causal):
    query_heads, key_heads, value_heads = split_heads(query, keys, values)
    scores = scores_of(query_heads, key_heads, bias, causal)
    row_max = jnp.max(scores, axis=-1, keepdims=True)
    exponent = jnp.exp(scores - row_max)
    total = jnp.sum(exponent, axis=-1, keepdims=True)
    probs = (exponent / total).astype(jnp.bfloat16)
    mixed = jnp.einsum("bgrij,bjgd->bigrd", probs, value_heads, preferred_element_type=jnp.float32)
    return (mixed.reshape(query.shape).astype(jnp.bfloat16), row_max + jnp.log(total))


def attend_backward(query, keys, values, bias, causal, log_total, grad_mixed):
    query_heads, key_heads, value_heads = split_heads(query, keys, values)
    probs = jnp.exp(scores_of(query_heads, key_heads, bias, causal) - log_total)
    grad_heads = grad_mixed.reshape(query_heads.shape)
    grad_probs = jnp.einsum(
        "bigrd,bjgd->bgrij", grad_heads, value_heads, preferred_element_type=jnp.float32
    )
    inner = jnp.sum(probs * grad_probs, axis=-1, keepdims=True)
    grad_scores = (probs * (grad_probs - inner)).astype(jnp.bfloat16)
    scale = DH ** (-0.5)
    grad_query = (
        jnp.einsum("bgrij,bjgd->bigrd", grad_scores, key_heads, preferred_element_type=jnp.float32)
        * scale
    ).astype(jnp.bfloat16)
    grad_keys = (
        jnp.einsum(
            "bgrij,bigrd->bjgd", grad_scores, query_heads, preferred_element_type=jnp.float32
        )
        * scale
    ).astype(jnp.bfloat16)
    grad_values = jnp.einsum(
        "bgrij,bigrd->bjgd",
        probs.astype(jnp.bfloat16),
        grad_heads,
        preferred_element_type=jnp.float32,
    ).astype(jnp.bfloat16)
    return (
        grad_query.reshape(query.shape),
        grad_keys.reshape(keys.shape),
        grad_values.reshape(values.shape),
        grad_scores,
    )


def forward(tokens, memory, weights, onehot, causal):
    gains, table, self_q, self_kv, self_out, cross_q, cross_kv, cross_out, gate_up, down = weights
    gain_rows = gains.astype(jnp.float32)
    start = tokens.astype(jnp.float32)
    normed_self = rms_norm(start, gain_rows[0]).astype(jnp.bfloat16)
    query_self = jnp.dot(normed_self, self_q, preferred_element_type=jnp.float32).astype(
        jnp.bfloat16
    )
    pair_self = jnp.dot(normed_self, flatten(self_kv), preferred_element_type=jnp.float32).astype(
        jnp.bfloat16
    )
    half = pair_self.shape[-1] // 2
    keys_self = pair_self[..., :half]
    values_self = pair_self[..., half:]
    groups = half // DH
    heads = table.shape[1]
    rows = tokens.shape[1]
    bias = jnp.einsum("ijn,nh->hij", onehot, table, preferred_element_type=jnp.float32).reshape(
        groups, heads // groups, rows, rows
    )
    mixed_self, log_self = attend_forward(query_self, keys_self, values_self, bias, causal)
    after_self = start + branch_total(
        jnp.dot(mixed_self, self_out, preferred_element_type=jnp.float32)
    )
    normed_cross = rms_norm(after_self, gain_rows[1]).astype(jnp.bfloat16)
    query_cross = jnp.dot(normed_cross, cross_q, preferred_element_type=jnp.float32).astype(
        jnp.bfloat16
    )
    pair_cross = jnp.dot(memory, flatten(cross_kv), preferred_element_type=jnp.float32).astype(
        jnp.bfloat16
    )
    keys_cross = pair_cross[..., :half]
    values_cross = pair_cross[..., half:]
    mixed_cross, log_cross = attend_forward(query_cross, keys_cross, values_cross, None, None)
    after_cross = after_self + branch_total(
        jnp.dot(mixed_cross, cross_out, preferred_element_type=jnp.float32)
    )
    normed_ffn = rms_norm(after_cross, gain_rows[2]).astype(jnp.bfloat16)
    joined = jnp.dot(normed_ffn, flatten(gate_up), preferred_element_type=jnp.float32)
    hidden_width = joined.shape[-1] // 2
    gate = joined[..., :hidden_width]
    up = joined[..., hidden_width:]
    hidden = gelu_product(gate, up).astype(jnp.bfloat16)
    output = after_cross + branch_total(jnp.dot(hidden, down, preferred_element_type=jnp.float32))
    saved = (
        start,
        after_self,
        after_cross,
        normed_self,
        query_self,
        keys_self,
        values_self,
        bias,
        mixed_self,
        log_self,
        normed_cross,
        query_cross,
        keys_cross,
        values_cross,
        mixed_cross,
        log_cross,
        normed_ffn,
        gate,
        up,
        hidden,
    )
    return (output, saved)


def backward(saved, grad_out, memory, weights, onehot, causal):
    (
        start,
        after_self,
        after_cross,
        normed_self,
        query_self,
        keys_self,
        values_self,
        bias,
        mixed_self,
        log_self,
        normed_cross,
        query_cross,
        keys_cross,
        values_cross,
        mixed_cross,
        log_cross,
        normed_ffn,
        gate,
        up,
        hidden,
    ) = saved
    gains, table, self_q, self_kv, self_out, cross_q, cross_kv, cross_out, gate_up, down = weights
    gain_rows = gains.astype(jnp.float32)
    grad_ffn = grad_out.astype(jnp.float32)
    rounded = grad_ffn.astype(jnp.bfloat16)
    down_grad = jnp.einsum("blf,bld->fd", hidden, rounded, preferred_element_type=jnp.float32)
    grad_hidden = jnp.einsum("bld,fd->blf", rounded, down, preferred_element_type=jnp.float32)
    _, pull = jax.vjp(gelu_product, gate, up)
    grad_gate, grad_up = pull(grad_hidden)
    grad_joined = jnp.concatenate([grad_gate, grad_up], axis=-1).astype(jnp.bfloat16)
    gate_up_grad = jnp.einsum(
        "bld,blf->df", normed_ffn, grad_joined, preferred_element_type=jnp.float32
    ).reshape(gate_up.shape)
    grad_normed = input_total(
        jnp.einsum("blf,df->bld", grad_joined, flatten(gate_up), preferred_element_type=jnp.float32)
    )
    _, pull = jax.vjp(rms_norm, after_cross, gain_rows[2])
    grad_residual, gain_ffn = pull(grad_normed)
    grad_cross = grad_ffn + grad_residual
    rounded = grad_cross.astype(jnp.bfloat16)
    cross_out_grad = jnp.einsum(
        "blh,bld->hd", mixed_cross, rounded, preferred_element_type=jnp.float32
    )
    grad_mixed = jnp.einsum(
        "bld,hd->blh", rounded, cross_out, preferred_element_type=jnp.float32
    ).astype(jnp.bfloat16)
    grad_query, grad_keys, grad_values, _ = attend_backward(
        query_cross, keys_cross, values_cross, None, None, log_cross, grad_mixed
    )
    grad_pair_cross = jnp.concatenate([grad_keys, grad_values], axis=-1)
    cross_q_grad = jnp.einsum(
        "bld,blh->dh", normed_cross, grad_query, preferred_element_type=jnp.float32
    )
    cross_kv_grad = jnp.einsum(
        "bsd,bsw->dw", memory, grad_pair_cross, preferred_element_type=jnp.float32
    ).reshape(cross_kv.shape)
    grad_normed = input_total(
        jnp.einsum("blh,dh->bld", grad_query, cross_q, preferred_element_type=jnp.float32)
    )
    _, pull = jax.vjp(rms_norm, after_self, gain_rows[1])
    grad_residual, gain_cross = pull(grad_normed)
    grad_self = grad_cross + grad_residual
    rounded = grad_self.astype(jnp.bfloat16)
    self_out_grad = jnp.einsum(
        "blh,bld->hd", mixed_self, rounded, preferred_element_type=jnp.float32
    )
    grad_mixed = jnp.einsum(
        "bld,hd->blh", rounded, self_out, preferred_element_type=jnp.float32
    ).astype(jnp.bfloat16)
    grad_query, grad_keys, grad_values, grad_scores = attend_backward(
        query_self, keys_self, values_self, bias, causal, log_self, grad_mixed
    )
    batch = grad_scores.shape[0]
    rows = grad_scores.shape[-1]
    table_grad = jnp.einsum(
        "ijn,bhij->nh",
        onehot,
        grad_scores.reshape(batch, -1, rows, rows),
        preferred_element_type=jnp.float32,
    )
    grad_pair = jnp.concatenate([grad_keys, grad_values], axis=-1)
    self_q_grad = jnp.einsum(
        "bld,blh->dh", normed_self, grad_query, preferred_element_type=jnp.float32
    )
    self_kv_grad = jnp.einsum(
        "bld,blw->dw", normed_self, grad_pair, preferred_element_type=jnp.float32
    ).reshape(self_kv.shape)
    grad_normed = input_total(
        jnp.einsum("blh,dh->bld", grad_query, self_q, preferred_element_type=jnp.float32)
        + jnp.einsum("blw,dw->bld", grad_pair, flatten(self_kv), preferred_element_type=jnp.float32)
    )
    _, pull = jax.vjp(rms_norm, start, gain_rows[0])
    grad_residual, gain_self = pull(grad_normed)
    grad_tokens = grad_self + grad_residual
    gains_grad = jnp.stack([gain_self, gain_cross, gain_ffn])
    grads = (
        gains_grad,
        table_grad,
        self_q_grad,
        self_kv_grad,
        self_out_grad,
        cross_q_grad,
        cross_kv_grad,
        cross_out_grad,
        gate_up_grad,
        down_grad,
    )
    return (grad_tokens, grad_pair_cross, grads)


def per_device(
    decoder_in,
    memory,
    buckets,
    norm_gains,
    rel_bias,
    self_q,
    self_kv,
    self_out,
    cross_q,
    cross_kv,
    cross_out,
    gate_up,
    down,
    cotangent,
):
    local = decoder_in.shape[0]
    rows = decoder_in.shape[1]
    per_batch = local // MICRO
    positions = jnp.arange(rows, dtype=jnp.int32)
    causal = positions[:, None] >= positions[None, :]
    onehot = (buckets[:, :, None] == jnp.arange(NB, dtype=jnp.int32)[None, None, :]).astype(
        jnp.bfloat16
    )
    weights = gather_weights(
        norm_gains, rel_bias, self_q, self_kv, self_out, cross_q, cross_kv, cross_out, gate_up, down
    )
    outputs = []
    token_grads = []
    memory_grads = []
    totals = None
    for index in range(MICRO):
        lower = index * per_batch
        upper = lower + per_batch
        memory_part = memory[lower:upper]
        output, saved = forward(decoder_in[lower:upper], memory_part, weights, onehot, causal)
        grad_tokens, grad_pair_cross, grads = backward(
            saved, cotangent[lower:upper], memory_part, weights, onehot, causal
        )
        memory_term = jnp.einsum(
            "bsw,dw->bsd", grad_pair_cross, flatten(weights[6]), preferred_element_type=jnp.float32
        )
        memory_part_grad = lax.psum_scatter(
            memory_term.astype(jnp.bfloat16), "tp", scatter_dimension=2, tiled=True
        )
        memory_grads.append(memory_part_grad)
        outputs.append(output.astype(jnp.bfloat16))
        token_grads.append(grad_tokens)
        grads = (
            lax.psum_scatter(
                grads[0].astype(jnp.bfloat16), ("seq", "fsdp"), scatter_dimension=1, tiled=True
            ).astype(jnp.float32),
            lax.psum_scatter(
                grads[1].astype(jnp.bfloat16), ("seq", "fsdp"), scatter_dimension=0, tiled=True
            ).astype(jnp.float32),
            lax.psum_scatter(
                grads[2].astype(jnp.bfloat16), ("seq", "fsdp"), scatter_dimension=0, tiled=True
            ).astype(jnp.float32),
            lax.psum_scatter(
                grads[3].astype(jnp.bfloat16), ("seq", "fsdp"), scatter_dimension=0, tiled=True
            ).astype(jnp.float32),
            lax.psum_scatter(
                grads[4].astype(jnp.bfloat16), ("seq", "fsdp"), scatter_dimension=1, tiled=True
            ).astype(jnp.float32),
            lax.psum_scatter(
                grads[5].astype(jnp.bfloat16), ("seq", "fsdp"), scatter_dimension=0, tiled=True
            ).astype(jnp.float32),
            lax.psum_scatter(
                grads[6].astype(jnp.bfloat16), ("seq", "fsdp"), scatter_dimension=0, tiled=True
            ).astype(jnp.float32),
            lax.psum_scatter(
                grads[7].astype(jnp.bfloat16), ("seq", "fsdp"), scatter_dimension=1, tiled=True
            ).astype(jnp.float32),
            lax.psum_scatter(
                grads[8].astype(jnp.bfloat16), ("seq", "fsdp"), scatter_dimension=0, tiled=True
            ).astype(jnp.float32),
            lax.psum_scatter(
                grads[9].astype(jnp.bfloat16), ("seq", "fsdp"), scatter_dimension=1, tiled=True
            ).astype(jnp.float32),
        )
        totals = grads if totals is None else jax.tree.map(jnp.add, totals, grads)
    return (
        jnp.concatenate(outputs, axis=0),
        jnp.concatenate(token_grads, axis=0),
        jnp.concatenate(memory_grads, axis=0),
        totals[0],
        totals[1],
        totals[2],
        totals[3],
        totals[4],
        totals[5],
        totals[6],
        totals[7],
        totals[8],
        totals[9],
    )


def solution(mesh):
    return jax.shard_map(
        per_device,
        mesh=mesh,
        in_specs=(
            P(("seq", "fsdp"), None, None),
            P(("seq", "fsdp"), None, None),
            P(),
            P(None, ("seq", "fsdp")),
            P(("seq", "fsdp"), "tp"),
            P(("seq", "fsdp"), "tp"),
            P(("seq", "fsdp"), None, "tp"),
            P("tp", ("seq", "fsdp")),
            P(("seq", "fsdp"), "tp"),
            P(("seq", "fsdp"), None, "tp"),
            P("tp", ("seq", "fsdp")),
            P(("seq", "fsdp"), None, "tp"),
            P("tp", ("seq", "fsdp")),
            P(("seq", "fsdp"), None, None),
        ),
        out_specs=(
            P(("seq", "fsdp"), None, None),
            P(("seq", "fsdp"), None, None),
            P(("seq", "fsdp"), None, "tp"),
            P(None, ("seq", "fsdp")),
            P(("seq", "fsdp"), "tp"),
            P(("seq", "fsdp"), "tp"),
            P(("seq", "fsdp"), None, "tp"),
            P("tp", ("seq", "fsdp")),
            P(("seq", "fsdp"), "tp"),
            P(("seq", "fsdp"), None, "tp"),
            P("tp", ("seq", "fsdp")),
            P(("seq", "fsdp"), None, "tp"),
            P("tp", ("seq", "fsdp")),
        ),
        check_vma=False,
    )
```

profile of v0, /device:TPU:0, one launch (start us, length us, event | category | flops | bytes accessed | tf_op | source)
XLA Modules:
  0.0 1106.7 jit_solution(3590226312965783500)
XLA Ops:
  10.3 13.7 %all_gather.30 = bf16[3,1024]{1,0:T(4,128)(2,1)S(1)} all-gather(bf16[3,128]{1,0:T(4,128)(2,1)} %param.17), channel_id=1, replica_groups=mesh['seq'=4,'tp'=4,'fsdp'=2] {'seq','fsdp'}, dimensions={1}, use_global_device_ids=true | all-gather | bytes 6912 | tf_op jit(solution)/shard_map/all_gather | solution.py:31
  24.0 15.1 %all_gather.32 = bf16[1024,256]{1,0:T(8,128)(2,1)S(1)} all-gather(bf16[128,256]{1,0:T(8,128)(2,1)} %param.19), channel_id=1, replica_groups=mesh['seq'=4,'tp'=4,'fsdp'=2] {'seq','fsdp'}, dimensions={0}, use_global_device_ids=true | all-gather | bytes 589824 | tf_op jit(solution)/shard_map/all_gather | solution.py:33
  42.2 14.9 %all_gather.31 = bf16[1024,2,128]{2,1,0:T(2,128)(2,1)S(1)} all-gather(bf16[128,2,128]{2,1,0:T(2,128)(2,1)S(1)} %copy-done.72), channel_id=1, replica_groups=mesh['seq'=4,'tp'=4,'fsdp'=2] {'seq','fsdp'}, dimensions={0}, use_global_device_ids=true | all-gather | bytes 589824 | tf_op jit(solution)/shard_map/all_gather | solution.py:34
  68.0 14.0 %all_gather.34 = bf16[256,1024]{1,0:T(8,128)(2,1)S(1)} all-gather(bf16[256,128]{1,0:T(8,128)(2,1)S(1)} %copy-done.73), channel_id=1, replica_groups=mesh['seq'=4,'tp'=4,'fsdp'=2] {'seq','fsdp'}, dimensions={1}, use_global_device_ids=true | all-gather | bytes 589824 | tf_op jit(solution)/shard_map/all_gather | solution.py:35
  86.6 15.2 %all_gather.35 = bf16[1024,2,128]{2,1,0:T(2,128)(2,1)S(1)} all-gather(bf16[128,2,128]{2,1,0:T(2,128)(2,1)} %param.23), channel_id=1, replica_groups=mesh['seq'=4,'tp'=4,'fsdp'=2] {'seq','fsdp'}, dimensions={0}, use_global_device_ids=true | all-gather | bytes 589824 | tf_op jit(solution)/shard_map/all_gather | solution.py:37
  114.3 15.8 %all_gather.36 = bf16[1024,256]{1,0:T(8,128)(2,1)} all-gather(bf16[128,256]{1,0:T(8,128)(2,1)S(1)} %copy-done.74), channel_id=1, replica_groups=mesh['seq'=4,'tp'=4,'fsdp'=2] {'seq','fsdp'}, dimensions={0}, use_global_device_ids=true | all-gather | bytes 589824 | tf_op jit(solution)/shard_map/all_gather | solution.py:36
  130.1 14.5 %all_gather.37 = bf16[256,1024]{1,0:T(8,128)(2,1)S(1)} all-gather(bf16[256,128]{1,0:T(8,128)(2,1)S(1)} %copy-done.75), channel_id=1, replica_groups=mesh['seq'=4,'tp'=4,'fsdp'=2] {'seq','fsdp'}, dimensions={1}, use_global_device_ids=true | all-gather | bytes 589824 | tf_op jit(solution)/shard_map/all_gather | solution.py:38
  169.0 10.6 all-reduce.26.cloned.1.call-start
  179.6 39.4 %all-reduce.28.cloned.1.call-done = (bf16[2,128,1024]{2,1,0:T(8,128)(2,1)}, bf16[2,128,1024]{2,1,0:T(8,128)(2,1)}) async-done(((bf16[2,128,1024]{2,1,0:T(8,128)(2,1)}, bf16[2,128,1024]{2,1,0:T(8,128)(2,1)}), (bf16[2,128,1024]{2,1,0:T(8,128)(2,1)}, bf16[2,128,1024]{2,1,0:T(8,128)(2,1)})) %all-reduce.28.cloned.1.call-update) | async-done | bytes 1048592 | tf_op jit(solution)/shard_map/psum | solution.py:45
  243.5 51.1 %all-reduce.26.cloned.1.call-done = (bf16[2,128,1024]{2,1,0:T(8,128)(2,1)}, bf16[2,128,1024]{2,1,0:T(8,128)(2,1)}) async-done(((bf16[2,128,1024]{2,1,0:T(8,128)(2,1)}, bf16[2,128,1024]{2,1,0:T(8,128)(2,1)}), (bf16[2,128,1024]{2,1,0:T(8,128)(2,1)}, bf16[2,128,1024]{2,1,0:T(8,128)(2,1)})) %all-reduce.26.cloned.1.call-update) | async-done | bytes 1048592 | tf_op jit(solution)/shard_map/psum | solution.py:49
  344.9 46.4 %all-reduce.24.cloned.1.call-done = (bf16[2,128,1024]{2,1,0:T(8,128)(2,1)}, bf16[2,128,1024]{2,1,0:T(8,128)(2,1)}) async-done(((bf16[2,128,1024]{2,1,0:T(8,128)(2,1)}, bf16[2,128,1024]{2,1,0:T(8,128)(2,1)}), (bf16[2,128,1024]{2,1,0:T(8,128)(2,1)}, bf16[2,128,1024]{2,1,0:T(8,128)(2,1)})) %all-reduce.24.cloned.1.call-update) | async-done | bytes 1048592 | tf_op jit(solution)/shard_map/psum | solution.py:49
  564.2 30.0 %all-reduce.6 = (bf16[32,4]{1,0:T(8,128)(2,1)S(1)}, bf16[32,4]{1,0:T(8,128)(2,1)S(1)}) all-reduce(bf16[32,4]{1,0:T(8,128)(2,1)S(1)} %fusion.118, bf16[32,4]{1,0:T(8,128)(2,1)S(1)} %fusion.117), channel_id=6, replica_groups=mesh['seq'=4,'tp'=4,'fsdp'=2] {'seq','fsdp'}, use_global_device_ids=true, to_apply=%region_47.48.clone | all-reduce | flops 256 | bytes 1024
  597.0 12.0 %reduce-scatter.67.cloned.1.call-done = bf16[128,704]{1,0:T(8,128)(2,1)} async-done(((bf16[1024,704]{1,0:T(8,128)(2,1)}), bf16[128,704]{1,0:T(8,128)(2,1)}) %reduce-scatter.67.cloned.1.call-update) | async-done | bytes 180240
  610.1 35.6 %reduce-scatter.65.cloned.1.call-done = bf16[128,704]{1,0:T(8,128)(2,1)} async-done(((bf16[1024,704]{1,0:T(8,128)(2,1)}), bf16[128,704]{1,0:T(8,128)(2,1)}) %reduce-scatter.65.cloned.1.call-update) | async-done | bytes 180240
  647.7 29.9 %reduce-scatter.53.cloned.1.call-done = bf16[128,256]{1,0:T(8,128)(2,1)} async-done(((bf16[1024,256]{1,0:T(8,128)(2,1)}), bf16[128,256]{1,0:T(8,128)(2,1)}) %reduce-scatter.53.cloned.1.call-update) | async-done | bytes 65552
  678.5 30.8 %reduce-scatter.55.cloned.1.call-done = bf16[128,256]{1,0:T(8,128)(2,1)} async-done(((bf16[1024,256]{1,0:T(8,128)(2,1)}), bf16[128,256]{1,0:T(8,128)(2,1)}) %reduce-scatter.55.cloned.1.call-update) | async-done | bytes 65552
  712.7 28.1 %reduce-scatter.41.cloned.1.call-done = bf16[128,256]{1,0:T(8,128)(2,1)} async-done(((bf16[1024,256]{1,0:T(8,128)(2,1)}), bf16[128,256]{1,0:T(8,128)(2,1)}) %reduce-scatter.41.cloned.1.call-update) | async-done | bytes 65552 | tf_op jit(solution)/shard_map/reduce_scatter | solution.py:356
  740.8 32.3 %reduce-scatter.43.cloned.1.call-done = bf16[128,256]{1,0:T(8,128)(2,1)} async-done(((bf16[1024,256]{1,0:T(8,128)(2,1)}), bf16[128,256]{1,0:T(8,128)(2,1)}) %reduce-scatter.43.cloned.1.call-update) | async-done | bytes 65552 | tf_op jit(solution)/shard_map/reduce_scatter | solution.py:356
  779.7 24.5 %reduce-scatter.49.cloned.1.call-done = bf16[128,3]{1,0:T(8,128)(2,1)} async-done(((bf16[1024,3]{1,0:T(8,128)(2,1)}), bf16[128,3]{1,0:T(8,128)(2,1)}) %reduce-scatter.49.cloned.1.call-update) | async-done | bytes 784
  805.0 30.8 %reduce-scatter.51.cloned.1.call-done = bf16[128,3]{1,0:T(8,128)(2,1)} async-done(((bf16[1024,3]{1,0:T(8,128)(2,1)}), bf16[128,3]{1,0:T(8,128)(2,1)}) %reduce-scatter.51.cloned.1.call-update) | async-done | bytes 784
  837.3 38.5 %reduce-scatter.63.cloned.1.call-done = bf16[128,1408]{1,0:T(8,128)(2,1)} async-done(((bf16[1024,1408]{1,0:T(8,128)(2,1)}), bf16[128,1408]{1,0:T(8,128)(2,1)}) %reduce-scatter.63.cloned.1.call-update) | async-done | bytes 360464
  877.0 39.3 %reduce-scatter.61.cloned.1.call-done = bf16[128,1408]{1,0:T(8,128)(2,1)} async-done(((bf16[1024,1408]{1,0:T(8,128)(2,1)}), bf16[128,1408]{1,0:T(8,128)(2,1)}) %reduce-scatter.61.cloned.1.call-update) | async-done | bytes 360464
  918.4 86.5 %reduce-scatter.39.cloned.1.call-done = bf16[2,2048,256]{2,1,0:T(8,128)(2,1)} async-done(((bf16[2,2048,1024]{2,1,0:T(8,128)(2,1)}), bf16[2,2048,256]{2,1,0:T(8,128)(2,1)}) %reduce-scatter.39.cloned.1.call-update) | async-done | bytes 2097168 | tf_op jit(solution)/shard_map/reduce_scatter | solution.py:343
  1004.9 89.3 %reduce-scatter.37.cloned.1.call-done = bf16[2,2048,256]{2,1,0:T(8,128)(2,1)} async-done(((bf16[2,2048,1024]{2,1,0:T(8,128)(2,1)}), bf16[2,2048,256]{2,1,0:T(8,128)(2,1)}) %reduce-scatter.37.cloned.1.call-update) | async-done | bytes 2097168 | tf_op jit(solution)/shard_map/reduce_scatter | solution.py:343
  (459 shorter events, 329.3 us)
Async XLA Ops:
  8.0 139.4 %all-reduce.30.cloned.1.call-start = ((), (), s32[]{:S(2)}) async-start(), calls=%async_computation.39 | async-start | bytes 2097152 | tf_op jit(solution)/shard_map/psum | solution.py:45
  86.6 132.4 %all-reduce.28.cloned.1.call-start = ((), (), s32[]{:S(2)}) async-start(), calls=%async_computation.38 | async-start | bytes 2097152 | tf_op jit(solution)/shard_map/psum | solution.py:45
  167.8 53.8 %all-gather.4.cloned.1.call-start = ((), (), s32[]{:S(2)}) async-start(), calls=%async_computation.16 | async-start | bytes 3244032 | tf_op jit(solution)/shard_map/all_gather | solution.py:39
  168.4 63.0 %all-gather.6.cloned.1.call-start = ((), (), s32[]{:S(2)}) async-start(), calls=%async_computation.17 | async-start | bytes 1622016 | tf_op jit(solution)/shard_map/all_gather | solution.py:40
  169.0 125.6 %all-reduce.26.cloned.1.call-start = ((), (), s32[]{:S(2)}) async-start(), calls=%async_computation.37 | async-start | bytes 2097152 | tf_op jit(solution)/shard_map/psum | solution.py:49
  243.4 147.9 %all-reduce.24.cloned.1.call-start = ((), (), s32[]{:S(2)}) async-start(), calls=%async_computation.36 | async-start | bytes 2097152 | tf_op jit(solution)/shard_map/psum | solution.py:49
  338.6 190.4 %all-reduce.22.cloned.1.call-start = ((), (), s32[]{:S(2)}) async-start(), calls=%async_computation.35 | async-start | bytes 4194304 | tf_op jit(solution)/shard_map/psum | solution.py:45
  436.1 122.6 %reduce-scatter.57.cloned.1.call-start = ((), (), s32[]{:S(2)}) async-start(), calls=%async_computation.28 | async-start | bytes 589824
  440.6 119.1 %reduce-scatter.59.cloned.1.call-start = ((), (), s32[]{:S(2)}) async-start(), calls=%async_computation.29 | async-start | bytes 589824
  445.4 150.1 %reduce-scatter.47.cloned.1.call-start = ((), (), s32[]{:S(2)}) async-start(), calls=%async_computation.23 | async-start | bytes 589824 | tf_op jit(solution)/shard_map/reduce_scatter | solution.py:365
  447.8 147.7 %reduce-scatter.45.cloned.1.call-start = ((), (), s32[]{:S(2)}) async-start(), calls=%async_computation.22 | async-start | bytes 589824 | tf_op jit(solution)/shard_map/reduce_scatter | solution.py:365
  450.3 158.7 %reduce-scatter.67.cloned.1.call-start = ((), (), s32[]{:S(2)}) async-start(), calls=%async_computation.33 | async-start | bytes 1769472
  455.8 190.0 %reduce-scatter.65.cloned.1.call-start = ((), (), s32[]{:S(2)}) async-start(), calls=%async_computation.32 | async-start | bytes 1769472
  461.2 216.3 %reduce-scatter.53.cloned.1.call-start = ((), (), s32[]{:S(2)}) async-start(), calls=%async_computation.26 | async-start | bytes 589824
  487.5 221.8 %reduce-scatter.55.cloned.1.call-start = ((), (), s32[]{:S(2)}) async-start(), calls=%async_computation.27 | async-start | bytes 589824
  509.2 201.1 %all-reduce.20.cloned.1.call-start = ((), (), s32[]{:S(2)}) async-start(), calls=%async_computation.34 | async-start | bytes 4194304
  526.0 214.9 %reduce-scatter.41.cloned.1.call-start = ((), (), s32[]{:S(2)}) async-start(), calls=%async_computation.20 | async-start | bytes 589824 | tf_op jit(solution)/shard_map/reduce_scatter | solution.py:356
  527.3 245.8 %reduce-scatter.43.cloned.1.call-start = ((), (), s32[]{:S(2)}) async-start(), calls=%async_computation.21 | async-start | bytes 589824 | tf_op jit(solution)/shard_map/reduce_scatter | solution.py:356
  528.7 275.5 %reduce-scatter.49.cloned.1.call-start = ((), (), s32[]{:S(2)}) async-start(), calls=%async_computation.24 | async-start | bytes 294912
  532.7 303.1 %reduce-scatter.51.cloned.1.call-start = ((), (), s32[]{:S(2)}) async-start(), calls=%async_computation.25 | async-start | bytes 294912
  533.7 342.0 %reduce-scatter.63.cloned.1.call-start = ((), (), s32[]{:S(2)}) async-start(), calls=%async_computation.31 | async-start | bytes 3244032
  537.6 378.6 %reduce-scatter.61.cloned.1.call-start = ((), (), s32[]{:S(2)}) async-start(), calls=%async_computation.30 | async-start | bytes 3244032
  541.5 463.4 %reduce-scatter.39.cloned.1.call-start = ((), (), s32[]{:S(2)}) async-start(), calls=%async_computation.19 | async-start | bytes 10485760 | tf_op jit(solution)/shard_map/reduce_scatter | solution.py:343
  548.8 545.4 %reduce-scatter.37.cloned.1.call-start = ((), (), s32[]{:S(2)}) async-start(), calls=%async_computation.18 | async-start | bytes 10485760 | tf_op jit(solution)/shard_map/reduce_scatter | solution.py:343
  (109 other events, 1575.7 us)
Sparse Core Ops, SparseCore 0:
  86.7 50.9 all-reduce.29
  168.0 50.9 all-reduce.27
  243.5 51.0 all-reduce.25
  338.8 52.4 all-reduce.23
  436.2 69.5 all-reduce.21
  526.1 75.4 all-reduce.19
Sparse Core Ops, SparseCore 1:
  169.9 35.4 all-gather.3
  206.8 24.6 all-gather.5
  440.7 31.2 reduce-scatter.56
  474.2 29.4 reduce-scatter.58
  505.9 29.3 reduce-scatter.46
  537.6 31.0 reduce-scatter.44
  571.5 37.5 reduce-scatter.66
  611.2 34.5 reduce-scatter.64
  647.9 29.6 reduce-scatter.52
  679.8 29.4 reduce-scatter.54
  711.4 29.3 reduce-scatter.40
  743.7 29.3 reduce-scatter.42
  775.2 28.9 reduce-scatter.48
  807.0 28.8 reduce-scatter.50
  838.7 37.0 reduce-scatter.62
  878.1 38.1 reduce-scatter.60
  919.3 85.5 reduce-scatter.38
  1007.9 86.2 reduce-scatter.36
where the time goes:
time: 1120 us; the launch traced here: 1110 us
  waiting for transfers between devices  622 us (56%)
  matrix products  177 us (16%)
  blocking collectives  142 us (13%)
  local copies, waits for them, and re-layouts  77 us (7%)
  other arithmetic  57.5 us (5%)
  between operations  19.1 us (2%)
  starting transfers between devices  12.4 us (1%)
    unnamed x35, waiting for transfers between devices  243 us
    reduce_scatter x2, waiting for transfers between devices, per_device(): lax.psum_scatter(memory_term.astype(jnp.bfloat16), 'tp', scatter_dimensio...  176 us
    psum x2, waiting for transfers between devices, input_total(): lax.psum(partial_value.astype(jnp.bfloat16), 'tp').astype(jnp.float32)  97.5 us
    reduce_scatter x2, waiting for transfers between devices, per_device(): lax.psum_scatter(grads[2].astype(jnp.bfloat16), ('seq', 'fsdp'), scatter_...  60.4 us
    unnamed x237, local copies, waits for them, and re-layouts  41 us
    psum x3, waiting for transfers between devices, branch_total(): lax.psum(partial_value.astype(jnp.bfloat16), 'tp').astype(jnp.float32)  39.4 us
    unnamed x1, blocking collectives  30 us
  transfers between devices with their start and end apart: 24, of which 16 were waited for; matrix products, arithmetic and copies ran while one was open for 16% of the time, Pallas kernels for 0%

commit v1 on v0

v1 whole, which is shorter than its diff:
```python
import jax
import jax.numpy as jnp
from jax import lax
from jax.sharding import PartitionSpec as P

DH = 64
NB = 32
EPSILON = 1e-06
MASKED = -1e30
F32 = jnp.float32
BF16 = jnp.bfloat16


def rms_norm(values, gain):
    return values * lax.rsqrt(jnp.mean(values * values, axis=-1, keepdims=True) + EPSILON) * gain


def gelu_product(gate, up):
    return jax.nn.gelu(gate, approximate=True) * up


def mm(a, b, dims):
    return lax.dot_general(a, b, (dims, ((), ())), preferred_element_type=F32)


def split_heads(query, keys, values):
    batch, rows, width = query.shape
    span = keys.shape[1]
    groups = keys.shape[2] // DH
    ratio = width // DH // groups
    return (
        query.reshape(batch, rows, groups, ratio, DH),
        keys.reshape(batch, span, groups, DH),
        values.reshape(batch, span, groups, DH),
    )


def scores_of(query_heads, key_heads, bias, causal):
    scores = jnp.einsum(
        "bigrd,bjgd->bgrij", query_heads, key_heads, preferred_element_type=F32
    ) * DH ** (-0.5)
    if bias is not None:
        scores = scores + bias
    if causal is not None:
        scores = jnp.where(causal, scores, MASKED)
    return scores


def attend_forward(query, keys, values, bias, causal):
    query_heads, key_heads, value_heads = split_heads(query, keys, values)
    scores = scores_of(query_heads, key_heads, bias, causal)
    row_max = jnp.max(scores, axis=-1, keepdims=True)
    exponent = jnp.exp(scores - row_max)
    total = jnp.sum(exponent, axis=-1, keepdims=True)
    probs = (exponent / total).astype(BF16)
    mixed = jnp.einsum("bgrij,bjgd->bigrd", probs, value_heads, preferred_element_type=F32)
    return (mixed.reshape(query.shape).astype(BF16), row_max + jnp.log(total))


def attend_backward(query, keys, values, bias, causal, log_total, grad_mixed):
    query_heads, key_heads, value_heads = split_heads(query, keys, values)
    probs = jnp.exp(scores_of(query_heads, key_heads, bias, causal) - log_total)
    grad_heads = grad_mixed.reshape(query_heads.shape)
    grad_probs = jnp.einsum("bigrd,bjgd->bgrij", grad_heads, value_heads, preferred_element_type=F32)
    inner = jnp.sum(probs * grad_probs, axis=-1, keepdims=True)
    grad_scores = (probs * (grad_probs - inner)).astype(BF16)
    scale = DH ** (-0.5)
    grad_query = (
        jnp.einsum("bgrij,bjgd->bigrd", grad_scores, key_heads, preferred_element_type=F32) * scale
    ).astype(BF16)
    grad_keys = (
        jnp.einsum("bgrij,bigrd->bjgd", grad_scores, query_heads, preferred_element_type=F32)
        * scale
    ).astype(BF16)
    grad_values = jnp.einsum(
        "bgrij,bigrd->bjgd", probs.astype(BF16), grad_heads, preferred_element_type=F32
    ).astype(BF16)
    return (
        grad_query.reshape(query.shape),
        grad_keys.reshape(keys.shape),
        grad_values.reshape(values.shape),
        grad_scores,
    )


def per_device(
    decoder_in,
    memory,
    buckets,
    norm_gains,
    rel_bias,
    self_q,
    self_kv,
    self_out,
    cross_q,
    cross_kv,
    cross_out,
    gate_up,
    down,
    cotangent,
    tp_size,
    seq_size,
):
    batch, rows, width = decoder_in.shape
    split = tp_size // batch
    if batch * split != tp_size or rows % split:
        raise ValueError("unsupported mesh")
    chunk = rows // split
    t = lax.axis_index("tp")
    f = lax.axis_index("fsdp")
    s = lax.axis_index("seq")
    zf = ("seq", "fsdp")

    def swap_tp(x, j):
        return lax.ppermute(x, "tp", [(i, i ^ j) for i in range(tp_size)])

    def swap_core(x):
        return lax.ppermute(x, "fsdp", [(0, 1), (1, 0)])

    def exchange(pieces):
        return [pieces[0]] + [swap_tp(pieces[j], j) for j in range(1, tp_size)]

    def spread(x):
        return [x] + [swap_tp(x, j) for j in range(1, tp_size)]

    def relative(x, member, count):
        return jnp.stack([lax.dynamic_index_in_dim(x, member ^ j, 0, False) for j in range(count)])

    def piece(x, j):
        part = x[j // split]
        if split == 1:
            return part
        return lax.dynamic_slice_in_dim(part, ((t % split) ^ (j % split)) * chunk, chunk, 0)

    def pieces_of(x):
        return [piece(x, j) for j in range(tp_size)]

    def whole_rows(pieces):
        if split == 1:
            return jnp.stack(pieces)
        out = []
        for b in range(batch):
            own = jnp.stack(pieces[b * split : (b + 1) * split])
            own = relative(own, t % split, split)
            out.append(own.reshape((rows,) + own.shape[2:]))
        return jnp.stack(out)

    def placed(pieces):
        out = jnp.zeros((tp_size,) + pieces[0].shape, pieces[0].dtype)
        for j in range(tp_size):
            out = lax.dynamic_update_index_in_dim(out, pieces[j], t ^ j, 0)
        return out

    def rejoin(own, other):
        first = jnp.where(f == 0, own, other)
        second = jnp.where(f == 0, other, own)
        full = jnp.stack([first, second], axis=1)
        return full.reshape(-1, full.shape[-1])

    shard = self_q.shape[0]
    extra = jnp.zeros((4, shard), BF16)
    extra = extra.at[:3].set(norm_gains)
    tb_rows, heads = rel_bias.shape
    extra = extra.at[3, : tb_rows * heads].set(rel_bias.reshape(-1))
    extra = lax.all_gather(extra, zf, axis=0, tiled=False)
    gains = jnp.transpose(extra[:, :3], (1, 0, 2)).reshape(3, -1).astype(F32)
    table = extra[:, 3, : tb_rows * heads].reshape(NB, heads)

    pack_full = jnp.stack(
        [
            jnp.concatenate([self_out.T, cross_kv.reshape(shard, -1)], axis=1),
            jnp.concatenate([cross_q, cross_out.T], axis=1),
        ]
    )
    got_full = lax.all_gather(pack_full, "seq", axis=0, tiled=False)
    pack_self = jnp.concatenate([self_q, self_kv.reshape(shard, -1)], axis=1)
    w_self = lax.all_gather(pack_self, zf, axis=0, tiled=True)
    pack_ffn = jnp.concatenate([gate_up.reshape(shard, -1), down.T], axis=1)
    w_ffn = lax.all_gather(pack_ffn, zf, axis=0, tiled=True)

    cols = self_q.shape[1]

    def full_pair(index):
        part = got_full[:, index]
        mine = spread(part)
        theirs = [swap_core(p) for p in mine]
        joined = [rejoin(a, b) for a, b in zip(mine, theirs)]
        first = jnp.concatenate([w[:, :cols] for w in joined], axis=1)
        second = jnp.concatenate([w[:, cols:] for w in joined], axis=1)
        return first, second

    w_so, w_ckv = full_pair(0)
    w_cq, w_co = full_pair(1)

    positions = jnp.arange(rows, dtype=jnp.int32)
    causal = positions[:, None] >= positions[None, :]
    onehot = (buckets[:, :, None] == jnp.arange(NB, dtype=jnp.int32)[None, None, :]).astype(BF16)
    kv_half = self_kv.shape[2]
    groups = kv_half // DH
    bias = jnp.einsum("ijn,nh->hij", onehot, table, preferred_element_type=F32).reshape(
        groups, heads // groups, rows, rows
    )

    tokens = relative(decoder_in, t // split, batch)
    start = tokens.astype(F32)
    normed_self = rms_norm(start, gains[0]).astype(BF16)
    proj = mm(normed_self, w_self, (((2,), (0,)))).astype(BF16)
    query_self = proj[..., :cols]
    keys_self = proj[..., cols : cols + kv_half]
    values_self = proj[..., cols + kv_half :]
    mixed_self, log_self = attend_forward(query_self, keys_self, values_self, bias, causal)
    o1 = jnp.concatenate(exchange(pieces_of(mixed_self)), axis=-1)

    x0 = piece(start, 0)
    x1 = x0 + mm(o1, w_so, ((1,), (1,)))
    n2 = rms_norm(x1, gains[1]).astype(BF16)
    q2 = mm(n2, w_cq, ((1,), (0,))).astype(BF16)
    own_memory = lax.dynamic_index_in_dim(memory, t // split, 0, False)
    kv2 = mm(own_memory, w_ckv, ((1,), (0,))).astype(BF16)
    span = kv2.shape[0]
    kv2 = kv2.reshape(span, tp_size, 2, kv_half)
    k2 = kv2[:, :, 0].reshape(1, span, -1)
    v2 = kv2[:, :, 1].reshape(1, span, -1)
    o2, log_cross = attend_forward(q2[None], k2, v2, None, None)
    x2 = x1 + mm(o2[0], w_co, ((1,), (1,)))
    n3 = rms_norm(x2, gains[2]).astype(BF16)

    n3_all = jnp.stack(spread(n3)).reshape(-1, width)
    ff2 = gate_up.shape[2] * 2
    hid = gate_up.shape[2]
    w_gu = w_ffn[:, :ff2]
    w_dn = w_ffn[:, ff2:]
    joined = mm(n3_all, w_gu, ((1,), (0,)))
    gate = joined[:, :hid]
    up = joined[:, hid:]
    hidden = gelu_product(gate, up).astype(BF16)
    out_part = mm(hidden, w_dn, ((1,), (1,))).astype(BF16).reshape(tp_size, chunk, width)

    cot = relative(cotangent.reshape(tp_size, chunk, width), t, tp_size)
    y3 = cot.reshape(-1, width)
    grad_hidden = mm(y3, w_dn, ((1,), (0,)))
    _, pull = jax.vjp(gelu_product, gate, up)
    grad_gate, grad_up = pull(grad_hidden)
    grad_joined = jnp.concatenate([grad_gate, grad_up], axis=-1).astype(BF16)
    dn3_part = mm(grad_joined, w_gu, ((1,), (1,))).astype(BF16).reshape(tp_size, chunk, width)

    def total(pieces):
        acc = pieces[0].astype(F32)
        for p in pieces[1:]:
            acc = acc + p.astype(F32)
        return acc

    dn3 = total(exchange([dn3_part[j] for j in range(tp_size)]))
    out = x2 + total(exchange([out_part[j] for j in range(tp_size)]))
    decoder_out = placed(spread(out.astype(BF16))).reshape(decoder_in.shape)

    gu_grad = mm(n3_all, grad_joined, ((0,), (0,))).astype(BF16)
    dn_grad = mm(y3, hidden, ((0,), (0,))).astype(BF16)
    ffn_grad = lax.psum_scatter(
        jnp.concatenate([gu_grad, dn_grad], axis=1), zf, scatter_dimension=0, tiled=True
    )

    e3 = cot[0].astype(F32)
    _, pull = jax.vjp(rms_norm, x2, gains[2])
    dv, dg2 = pull(dn3)
    e2 = e3 + dv
    y2 = e2.astype(BF16)
    do2 = mm(y2, w_co, ((1,), (0,))).astype(BF16)
    dq2, dk2, dv2, _ = attend_backward(q2[None], k2, v2, None, None, log_cross, do2[None])
    dq2 = dq2[0]
    dkv2 = jnp.stack(
        [dk2[0].reshape(span, tp_size, kv_half), dv2[0].reshape(span, tp_size, kv_half)], axis=2
    ).reshape(span, -1)
    dn2 = mm(dq2, w_cq, ((1,), (1,)))
    _, pull = jax.vjp(rms_norm, x1, gains[1])
    dv, dg1 = pull(dn2)
    e1 = e2 + dv
    y1 = e1.astype(BF16)
    do1_full = mm(y1, w_so, ((1,), (0,))).astype(BF16)
    do1 = whole_rows(exchange([do1_full[:, j * cols : (j + 1) * cols] for j in range(tp_size)]))

    quarter = width // tp_size
    w_rows = w_ckv.reshape(tp_size, quarter, -1)
    mem_pieces = []
    for j in range(tp_size):
        w_j = lax.dynamic_index_in_dim(w_rows, t ^ j, 0, False)
        mem_pieces.append(mm(dkv2, w_j, ((1,), (1,))).astype(BF16))
    mem_got = exchange(mem_pieces)
    memory_grad = jnp.zeros((batch,) + mem_got[0].shape, BF16)
    for b in range(batch):
        own = mem_got[b * split]
        if split > 1:
            own = total(mem_got[b * split : (b + 1) * split]).astype(BF16)
        memory_grad = lax.dynamic_update_index_in_dim(memory_grad, own, (t // split) ^ b, 0)

    def core_sum(grad):
        g = grad.reshape(seq_size, 2, shard, -1)
        mine = lax.dynamic_index_in_dim(g, f, 1, False)
        theirs = lax.dynamic_index_in_dim(g, 1 - f, 1, False)
        return (mine.astype(F32) + swap_core(theirs).astype(F32)).astype(BF16)

    def tp_sum(parts):
        pieces = [
            jnp.concatenate([p[..., j * cols : (j + 1) * cols] for p in parts], axis=-1)
            for j in range(tp_size)
        ]
        return total(exchange(pieces)).astype(BF16)

    g_co = core_sum(mm(y2, o2[0], ((0,), (0,))).astype(BF16))
    g_cq = core_sum(mm(n2, dq2, ((0,), (0,))).astype(BF16))
    g_ckv = core_sum(mm(own_memory, dkv2, ((0,), (0,))).astype(BF16))
    g_so = core_sum(mm(y1, o1, ((0,), (0,))).astype(BF16))
    full_grad = tp_sum([g_co, g_cq, g_ckv, g_so])
    full_grad = lax.psum_scatter(full_grad, "seq", scatter_dimension=0, tiled=False)

    dq1, dk1, dv1, ds1 = attend_backward(
        query_self, keys_self, values_self, bias, causal, log_self, do1
    )
    table_grad = jnp.einsum(
        "ijn,bhij->nh", onehot, ds1.reshape(batch, -1, rows, rows), preferred_element_type=F32
    )
    dproj = jnp.concatenate([dq1, dk1, dv1], axis=-1)
    dn1_part = mm(dproj, w_self, ((2,), (1,))).astype(BF16)
    self_grad = lax.psum_scatter(
        mm(normed_self.reshape(-1, width), dproj.reshape(-1, dproj.shape[-1]), ((0,), (0,))).astype(
            BF16
        ),
        zf,
        scatter_dimension=0,
        tiled=True,
    )
    dn1 = total(exchange(pieces_of(dn1_part)))
    _, pull = jax.vjp(rms_norm, x0, gains[0])
    dv, dg0 = pull(dn1)
    decoder_grad = placed(spread((e1 + dv).astype(BF16))).reshape(decoder_in.shape).astype(F32)

    small = jnp.stack([dg0, dg1, dg2, jnp.pad(table_grad.reshape(-1), (0, width - NB * heads))])
    small = lax.all_gather(small, ("seq", "fsdp", "tp"), axis=0, tiled=False)
    place = s * 2 + f
    gains_grad = lax.dynamic_slice_in_dim(jnp.sum(small[:, :3], axis=0), place * shard, shard, 1)
    tables = small[:, 3, : NB * heads].reshape(-1, tp_size, NB * heads)
    tables = jnp.sum(lax.dynamic_index_in_dim(tables, t, 1, False), axis=0).reshape(NB, heads)
    bias_grad = lax.dynamic_slice_in_dim(tables, place * tb_rows, tb_rows, 0)

    full_grad = full_grad.astype(F32)
    self_grad = self_grad.astype(F32)
    ffn_grad = ffn_grad.astype(F32)
    return (
        decoder_out,
        decoder_grad,
        memory_grad,
        gains_grad,
        bias_grad,
        self_grad[:, :cols],
        self_grad[:, cols:].reshape(self_kv.shape),
        full_grad[:, 3 * cols :].T,
        full_grad[:, cols : 2 * cols],
        full_grad[:, 2 * cols : 3 * cols].reshape(cross_kv.shape),
        full_grad[:, :cols].T,
        ffn_grad[:, :ff2].reshape(gate_up.shape),
        ffn_grad[:, ff2:].T,
    )


def solution(mesh):
    tp_size = mesh.shape["tp"]
    seq_size = mesh.shape["seq"]

    def body(*args):
        return per_device(*args, tp_size=tp_size, seq_size=seq_size)

    both = ("seq", "fsdp")
    token = P(both, None, None)
    weight = P(both, "tp")
    paired = P(both, None, "tp")
    turned = P("tp", both)
    return jax.shard_map(
        body,
        mesh=mesh,
        in_specs=(
            token,
            token,
            P(),
            P(None, both),
            weight,
            weight,
            paired,
            turned,
            weight,
            paired,
            turned,
            paired,
            turned,
            token,
        ),
        out_specs=(
            token,
            token,
            P(both, None, "tp"),
            P(None, both),
            weight,
            weight,
            paired,
            turned,
            weight,
            paired,
            turned,
            paired,
            turned,
        ),
        check_vma=False,
    )
```

time: 1120 us -> 560 us (0.50)
  waiting for transfers between devices: 622 us -> 136 us
  matrix products: 177 us -> 109 us
  blocking collectives: 142 us -> 96.6 us
  starting transfers between devices: 12.4 us -> 45.6 us
    unnamed x35 -> x6, waiting for transfers between devices: 243 us -> 0.1 us
    reduce_scatter x6 -> x3, waiting for transfers between devices: 236 us -> 0.01 us  [the longest x1 0.01 us: per_device(): lax.psum_scatter(mm(normed_self.reshape(-1, width), dproj.reshape(-1, dpr...]
    psum x5 -> x0, waiting for transfers between devices: 137 us -> none  [the longest x2 97.5 us: input_total(): lax.psum(partial_value.astype(jnp.bfloat16), 'tp').astype(jnp.float32)]
    ppermute x0 -> x48, waiting for transfers between devices: none -> 110 us  [the longest x36 110 us: swap_tp(): return lax.ppermute(x, 'tp', [(i, i ^ j) for i in range(tp_size)])]
    dot_general x55 -> x28, matrix products: 136 us -> 72.8 us  [the longest x24 60.5 us: mm(): return lax.dot_general(a, b, (dims, ((), ())), preferred_element_type=F32)]
    ppermute x0 -> x48, starting transfers between devices: none -> 45.4 us  [the longest x36 42.6 us: swap_tp(): return lax.ppermute(x, 'tp', [(i, i ^ j) for i in range(tp_size)])]
    unnamed x1 -> x0, blocking collectives: 30 us -> none
    another operation x2 -> x22, other arithmetic: 0.04 us -> 24.8 us  [backward(): gains_grad = jnp.stack([gain_self, gain_cross, gain_ffn])]
  transfers between devices with their start and end apart: 24 -> 54, of which waited for: 16 -> 15; matrix products, arithmetic and copies ran while one was open for 16% -> 33% of each run, Pallas kernels for 0% -> 0%
where the time goes in v1:
time: 560 us; the launch traced here: 552 us
  waiting for transfers between devices  136 us (24%)
  matrix products  109 us (19%)
  blocking collectives  96.6 us (17%)
  local copies, waits for them, and re-layouts  85.9 us (15%)
  other arithmetic  62.1 us (11%)
  starting transfers between devices  45.6 us (8%)
  between operations  16.4 us (3%)
    ppermute x36, waiting for transfers between devices, swap_tp(): return lax.ppermute(x, 'tp', [(i, i ^ j) for i in range(tp_size)])  110 us
    all_gather x1, blocking collectives, per_device(): small = lax.all_gather(small, ('seq', 'fsdp', 'tp'), axis=0, tiled=False)  83.1 us
    dot_general x24, matrix products, mm(): return lax.dot_general(a, b, (dims, ((), ())), preferred_element_type=F32)  60.5 us
    ppermute x36, starting transfers between devices, swap_tp(): return lax.ppermute(x, 'tp', [(i, i ^ j) for i in range(tp_size)])  42.6 us
    unnamed x223, local copies, waits for them, and re-layouts  20.3 us
    all_gather x1, waiting for transfers between devices, per_device(): w_self = lax.all_gather(pack_self, zf, axis=0, tiled=True)  17.2 us
    all_gather x1, blocking collectives, per_device(): extra = lax.all_gather(extra, zf, axis=0, tiled=False)  13.5 us
    dot_general x2, matrix products, attend_backward(): jnp.einsum('bigrd,bjgd->bgrij', grad_heads, value_heads, preferred_elemen...  13.2 us
  transfers between devices with their start and end apart: 54, of which 15 were waited for; matrix products, arithmetic and copies ran while one was open for 33% of the time, Pallas kernels for 0%

profile of v1, /device:TPU:0, one launch (start us, length us, event | category | flops | bytes accessed | tf_op | source)
XLA Modules:
  0.0 551.6 jit_solution(9025525953042338345)
XLA Ops:
  15.4 13.5 %all_gather.28 = bf16[8,4,128]{2,1,0:T(4,128)(2,1)S(1)} all-gather(bf16[1,4,128]{2,1,0:T(4,128)(2,1)S(1)} %scatter.9), channel_id=1, replica_groups=mesh['seq'=4,'tp'=4,'fsdp'=2] {'seq','fsdp'}, dimensions={0}, use_global_device_ids=true | all-gather | bytes 9216 | tf_op jit(solution)/shard_map/all_gather | solution.py:165
  34.0 8.6 %all-gather.11.cloned.1.call-done = bf16[8,128,512]{2,1,0:T(8,128)(2,1)} async-done(((bf16[2,128,512]{2,1,0:T(8,128)(2,1)}), bf16[8,128,512]{2,1,0:T(8,128)(2,1)}) %all-gather.11.cloned.1.call-update) | async-done | bytes 1048592 | tf_op jit(solution)/shard_map/all_gather | solution.py:175
  48.9 17.2 %all-gather.7.cloned.1.call-done = bf16[1024,512]{1,0:T(8,128)(2,1)} async-done(((bf16[128,512]{1,0:T(8,128)(2,1)}), bf16[1024,512]{1,0:T(8,128)(2,1)}) %all-gather.7.cloned.1.call-update) | async-done | bytes 1048592 | tf_op jit(solution)/shard_map/all_gather | solution.py:177
  93.7 8.1 %collective-permute-done.13 = bf16[4,128,512]{2,1,0:T(8,128)(2,1)S(1)} collective-permute-done((bf16[4,128,512]{2,1,0:T(8,128)(2,1)}, bf16[4,128,512]{2,1,0:T(8,128)(2,1)S(1)}, u32[]{:S(2)}, u32[]{:S(2)}) %collective-permute-start.13) | collective-permute-done | bytes 524320 | tf_op jit(solution)/shard_map/ppermute | solution.py:115
  112.4 7.5 %fusion.21 = bf16[2048,1024]{0,1:T(8,128)(2,1)S(1)} fusion(bf16[4,2048,1024]{2,1,0:T(8,128)(2,1)} %param.19, s32[]{:T(128)S(6)} %select_n.140, bf16[1024,256]{1,0:T(8,128)(2,1)S(1)} %get-tuple-element.184, bf16[1024,256]{1,0:T(8,128)(2,1)S(1)} %copy-done.39, bf16[1024,256]{1,0:T(8,128)(2,1)S(1)} %copy-done.40, bf16[1024,256]{1,0:T(8,128)(2,1)S(1)} %get-tuple-element.178), kind=kOutput, calls=%fused_computation.31 | convolution fusion | flops 4305453056 | bytes 10485764 | tf_op jit(solution)/shard_map/dot_general | solution.py:23
  120.3 8.2 %bitcast_reduce_fusion = (f32[8,2,128]{2,1,0:T(2,128)S(1)}, f32[8,2048,128,2]{2,1,3,0:T(8,128)}) fusion(bf16[2048,8,64,1]{0,2,3,1:T(8,128)(2,1)S(1)} %bitcast.415, bf16[128,8,2,64]{0,3,2,1:T(8,128)(2,1)S(1)} %bitcast.424), kind=kOutput, calls=%fused_computation.7 | convolution fusion | flops 545257472 | bytes 19144704 | tf_op jit(solution)/shard_map/bigrd,bjgd->bgrij/dot_general | solution.py:39
  128.5 8.6 %fusion.5 = f32[8,2,128]{2,1,0:T(2,128)S(1)} fusion(f32[8,2048,128,2]{2,1,3,0:T(8,128)} %get-tuple-element.220, f32[8,2,128]{2,1,0:T(2,128)S(1)} %get-tuple-element.219), kind=kLoop, calls=%fused_computation.11 | loop fusion | flops 12580864 | bytes 16793600 | tf_op jit(solution)/shard_map/reduce_sum | solution.py:54
  137.1 7.7 %fusion.63 = bf16[8,64,2,128]{3,1,2,0:T(8,128)(2,1)S(1)} fusion(bf16[2048,8,64,1]{0,2,3,1:T(8,128)(2,1)S(1)} %bitcast.421, f32[8,2,128]{2,1,0:T(2,128)S(1)} %fusion.5, f32[8,2,128]{2,1,0:T(2,128)S(1)} %get-tuple-element.219, f32[8,2048,128,2]{2,1,3,0:T(8,128)} %get-tuple-element.220), kind=kOutput, calls=%fused_computation.104 | convolution fusion | flops 553779200 | bytes 19152896 | tf_op jit(solution)/shard_map/bgrij,bjgd->bigrd/dot_general | solution.py:56
  151.5 5.4 collective-permute-done.19
  156.9 4.8 collective-permute-done.18
  163.8 4.1 fusion.30
  176.4 6.6 %collective-permute-done.28 = bf16[128,1024]{1,0:T(8,128)(2,1)S(1)} collective-permute-done((bf16[128,1024]{1,0:T(8,128)(2,1)S(1)}, bf16[128,1024]{1,0:T(8,128)(2,1)S(1)}, u32[]{:S(2)}, u32[]{:S(2)}) %collective-permute-start.28) | collective-permute-done | bytes 262176 | tf_op jit(solution)/shard_map/ppermute | solution.py:115
  182.9 4.6 collective-permute-done.27
  191.6 11.9 %fusion = (f32[8,2,128]{2,1,0:T(2,128)S(1)}, f32[8,2048,128,2]{2,1,3,0:T(8,128)}) fusion(f32[8,2048,128,2]{2,1,3,0:T(8,128)} %get-tuple-element.220, f32[8,2,128]{2,1,0:T(2,128)S(1)} %bitcast.490, bf16[2048,8,64,1]{0,2,3,1:T(8,128)(2,1)} %bitcast.422, bf16[128,8,2,64]{0,3,2,1:T(8,128)(2,1)} %bitcast.442), kind=kOutput, calls=%fused_computation.2 | convolution fusion | flops 553646080 | bytes 35930112 | tf_op jit(solution)/shard_map/bigrd,bjgd->bgrij/dot_general | solution.py:64
  203.5 10.1 %bitcast_convert_fusion = bf16[8,64,2048]{2,1,0:T(8,128)(2,1)} fusion(bf16[128,8,2,64]{0,3,2,1:T(8,128)(2,1)S(1)} %bitcast.443, f32[8,2048,128,2]{2,1,3,0:T(8,128)} %get-tuple-element.220, f32[8,2,128]{2,1,0:T(2,128)S(1)} %bitcast.491), kind=kOutput, calls=%fused_computation.23 | convolution fusion | flops 550502400 | bytes 19144704 | tf_op jit(solution)/shard_map/bgrij,bigrd->bjgd/dot_general | solution.py:75
  213.6 12.0 %fusion.10 = bf16[8,2,128,2048]{2,3,1,0:T(8,128)(2,1)S(1)} fusion(f32[8,2048,128,2]{2,1,3,0:T(8,128)} %get-tuple-element.224, f32[8,2048,128,2]{2,1,3,0:T(8,128)} %get-tuple-element.220, f32[8,2,128]{2,1,0:T(2,128)S(1)} %get-tuple-element.223, f32[8,2,128]{2,1,0:T(2,128)S(1)} %bitcast.492), kind=kLoop, calls=%fused_computation.15 | loop fusion | flops 20971520 | bytes 41959424 | tf_op jit(solution)/shard_map/reshape.150
  248.1 8.6 %fusion.42 = bf16[1024,1024]{1,0:T(8,128)(2,1)S(1)} fusion(bf16[2048,1024]{0,1:T(8,128)(2,1)S(1)} %bitcast.428, bf16[4,2048,1024]{2,1,0:T(8,128)(2,1)} %param.19, s32[]{:T(128)S(6)} %select_n.140), kind=kOutput, calls=%fused_computation.66 | convolution fusion | flops 4296015872 | bytes 10485764 | tf_op jit(solution)/shard_map/dot_general | solution.py:23
  297.9 23.2 %collective-permute-done.47 = bf16[4,128,1024]{1,2,0:T(8,128)(2,1)S(1)} collective-permute-done((bf16[4,128,1024]{1,2,0:T(8,128)(2,1)S(1)}, bf16[4,128,1024]{1,2,0:T(8,128)(2,1)S(1)}, u32[]{:S(2)}, u32[]{:S(2)}) %collective-permute-start.47) | collective-permute-done | bytes 1048608 | tf_op jit(solution)/shard_map/ppermute | solution.py:115
  321.1 21.5 %collective-permute-done.46 = bf16[4,128,1024]{1,2,0:T(8,128)(2,1)S(1)} collective-permute-done((bf16[4,128,1024]{1,2,0:T(8,128)(2,1)S(1)}, bf16[4,128,1024]{1,2,0:T(8,128)(2,1)S(1)}, u32[]{:S(2)}, u32[]{:S(2)}) %collective-permute-start.46) | collective-permute-done | bytes 1048608 | tf_op jit(solution)/shard_map/ppermute | solution.py:115
  367.1 4.9 collective-permute-done.22
  371.9 4.7 collective-permute-done.21
  410.6 11.7 %collective-permute-done.34 = bf16[128,1024]{1,0:T(8,128)(2,1)S(1)} collective-permute-done((bf16[128,1024]{1,0:T(8,128)(2,1)}, bf16[128,1024]{1,0:T(8,128)(2,1)S(1)}, u32[]{:S(2)}, u32[]{:S(2)}) %collective-permute-start.34) | collective-permute-done | bytes 262176 | tf_op jit(solution)/shard_map/ppermute | solution.py:115
  433.5 83.1 %all-gather.2 = f32[32,4,1024]{2,1,0:T(4,128)S(1)} all-gather(f32[1,4,1024]{2,1,0:T(4,128)S(1)} %maximum_bitcast_fusion.2), channel_id=3, replica_groups=mesh['seq'=4,'tp'=4,'fsdp'=2] {'seq','fsdp','tp'}, dimensions={0}, use_global_device_ids=true | all-gather | bytes 540672 | tf_op jit(solution)/shard_map/all_gather | solution.py:338
  519.4 5.8 %collective-permute-done.37 = bf16[128,1024]{1,0:T(8,128)(2,1)S(1)} collective-permute-done((bf16[128,1024]{1,0:T(8,128)(2,1)S(1)}, bf16[128,1024]{1,0:T(8,128)(2,1)S(1)}, u32[]{:S(2)}, u32[]{:S(2)}) %collective-permute-start.37) | collective-permute-done | bytes 262176 | tf_op jit(solution)/shard_map/ppermute | solution.py:115
  (502 shorter events, 232.8 us)
Async XLA Ops:
  7.2 35.4 %all-gather.11.cloned.1.call-start = ((), (), s32[]{:S(2)}) async-start(), calls=%async_computation.8 | async-start | bytes 1310720 | tf_op jit(solution)/shard_map/all_gather | solution.py:175
  11.7 54.3 %all-gather.7.cloned.1.call-start = ((), (), s32[]{:S(2)}) async-start(), calls=%async_computation.3 | async-start | bytes 1179648 | tf_op jit(solution)/shard_map/all_gather | solution.py:177
  14.2 149.6 %all-gather.9.cloned.1.call-start = ((), (), s32[]{:S(2)}) async-start(), calls=%async_computation.4 | async-start | bytes 4866048 | tf_op jit(solution)/shard_map/all_gather | solution.py:179
  15.1 520.5 %reduce-scatter.4.cloned.1.call-start = ((), (), s32[]{:S(2)}) async-start(), calls=%async_computation.5 | async-start | bytes 1179648 | tf_op jit(solution)/shard_map/reduce_scatter | solution.py:324
  44.9 34.6 %collective-permute-start.8 = (bf16[4,128,512]{2,1,0:T(8,128)(2,1)}, bf16[4,128,512]{2,1,0:T(8,128)(2,1)}, u32[]{:S(2)}, u32[]{:S(2)}) collective-permute-start(bf16[4,128,512]{2,1,0:T(8,128)(2,1)} %get-tuple-element.177), channel_id=1, source_target_pairs={{0,6},{2,4},{4,2},{6,0},{1,7},{3,5},{5,3},{7,1},{8,14},{10,12},{12... | collective-permute-start | bytes 1572872 | tf_op jit(solution)/shard_map/ppermute | solution.py:115
  47.3 32.3 %collective-permute-start.6 = (bf16[4,128,512]{2,1,0:T(8,128)(2,1)}, bf16[4,128,512]{2,1,0:T(8,128)(2,1)}, u32[]{:S(2)}, u32[]{:S(2)}) collective-permute-start(bf16[4,128,512]{2,1,0:T(8,128)(2,1)} %get-tuple-element.177), channel_id=1, source_target_pairs={{0,4},{2,6},{4,0},{6,2},{1,5},{3,7},{5,1},{7,3},{8,12},{10,14},{12... | collective-permute-start | bytes 1572872 | tf_op jit(solution)/shard_map/ppermute | solution.py:115
  47.8 33.3 %collective-permute-start.4 = (bf16[4,128,512]{2,1,0:T(8,128)(2,1)}, bf16[4,128,512]{2,1,0:T(8,128)(2,1)}, u32[]{:S(2)}, u32[]{:S(2)}) collective-permute-start(bf16[4,128,512]{2,1,0:T(8,128)(2,1)} %get-tuple-element.177), channel_id=1, source_target_pairs={{0,2},{2,0},{4,6},{6,4},{1,3},{3,1},{5,7},{7,5},{8,10},{10,8},{12,... | collective-permute-start | bytes 1572872 | tf_op jit(solution)/shard_map/ppermute | solution.py:115
  48.4 28.7 %collective-permute-start.3 = (bf16[4,128,512]{2,1,0:T(8,128)(2,1)}, bf16[4,128,512]{2,1,0:T(8,128)(2,1)}, u32[]{:S(2)}, u32[]{:S(2)}) collective-permute-start(bf16[4,128,512]{2,1,0:T(8,128)(2,1)} %get-tuple-element.177), channel_id=1, source_target_pairs={{0,1},{1,0},{2,3},{3,2},{4,5},{5,4},{6,7},{7,6},{8,9},{9,8},{10,11... | collective-permute-start | bytes 1572872 | tf_op jit(solution)/shard_map/ppermute | solution.py:118
  48.4 26.2 %collective-permute-start.10 = (bf16[4,128,512]{2,1,0:T(8,128)(2,1)}, bf16[4,128,512]{2,1,0:T(8,128)(2,1)}, u32[]{:S(2)}, u32[]{:S(2)}) collective-permute-start(bf16[4,128,512]{2,1,0:T(8,128)(2,1)} %get-tuple-element.176), channel_id=1, source_target_pairs={{0,1},{1,0},{2,3},{3,2},{4,5},{5,4},{6,7},{7,6},{8,9},{9,8},{10,11... | collective-permute-start | bytes 1572872 | tf_op jit(solution)/shard_map/ppermute | solution.py:118
  238.0 37.4 %collective-permute-start.31 = (bf16[128,256]{1,0:T(8,128)(2,1)}, bf16[128,256]{1,0:T(8,128)(2,1)}, u32[]{:S(2)}, u32[]{:S(2)}) collective-permute-start(bf16[128,256]{1,0:T(8,128)(2,1)} %get-tuple-element.203), channel_id=1, source_target_pairs={{0,6},{2,4},{4,2},{6,0},{1,7},{3,5},{5,3},{7,1},{8,14},{10,12},{12... | collective-permute-start | bytes 196616 | tf_op jit(solution)/shard_map/ppermute | solution.py:115
  239.5 36.9 %collective-permute-start.30 = (bf16[128,256]{1,0:T(8,128)(2,1)}, bf16[128,256]{1,0:T(8,128)(2,1)}, u32[]{:S(2)}, u32[]{:S(2)}) collective-permute-start(bf16[128,256]{1,0:T(8,128)(2,1)} %get-tuple-element.204), channel_id=1, source_target_pairs={{0,4},{2,6},{4,0},{6,2},{1,5},{3,7},{5,1},{7,3},{8,12},{10,14},{12... | collective-permute-start | bytes 196616 | tf_op jit(solution)/shard_map/ppermute | solution.py:115
  240.1 37.8 %collective-permute-start.29 = (bf16[128,256]{1,0:T(8,128)(2,1)}, bf16[128,256]{1,0:T(8,128)(2,1)S(1)}, u32[]{:S(2)}, u32[]{:S(2)}) collective-permute-start(bf16[128,256]{1,0:T(8,128)(2,1)} %get-tuple-element.205), channel_id=1, source_target_pairs={{0,2},{2,0},{4,6},{6,4},{1,3},{3,1},{5,7},{7,5},{8,10},{10,8},{12,... | collective-permute-start | bytes 196616 | tf_op jit(solution)/shard_map/ppermute | solution.py:115
  246.1 41.3 %collective-permute-start.44 = (bf16[4,128,1024]{1,2,0:T(8,128)(2,1)}, bf16[4,128,1024]{1,2,0:T(8,128)(2,1)}, u32[]{:S(2)}, u32[]{:S(2)}) collective-permute-start(bf16[4,128,1024]{1,2,0:T(8,128)(2,1)} %bitcast.458), channel_id=1, source_target_pairs={{0,1},{1,0},{2,3},{3,2},{4,5},{5,4},{6,7},{7,6},{8,9},{9,8},{10,11... | collective-permute-start | bytes 3145736 | tf_op jit(solution)/shard_map/ppermute | solution.py:118
  260.8 28.3 %collective-permute-start.43 = (bf16[4,128,1024]{1,2,0:T(8,128)(2,1)}, bf16[4,128,1024]{1,2,0:T(8,128)(2,1)}, u32[]{:S(2)}, u32[]{:S(2)}) collective-permute-start(bf16[4,128,1024]{1,2,0:T(8,128)(2,1)} %bitcast.459), channel_id=1, source_target_pairs={{0,1},{1,0},{2,3},{3,2},{4,5},{5,4},{6,7},{7,6},{8,9},{9,8},{10,11... | collective-permute-start | bytes 3145736 | tf_op jit(solution)/shard_map/ppermute | solution.py:118
  287.3 250.5 %reduce-scatter.6.cloned.1.call-start = ((), (), s32[]{:S(2)}) async-start(), calls=%async_computation.6 | async-start | bytes 1310720 | tf_op jit(solution)/shard_map/reduce_scatter | solution.py:314
  294.1 27.0 %collective-permute-start.47 = (bf16[4,128,1024]{1,2,0:T(8,128)(2,1)S(1)}, bf16[4,128,1024]{1,2,0:T(8,128)(2,1)S(1)}, u32[]{:S(2)}, u32[]{:S(2)}) collective-permute-start(bf16[4,128,1024]{1,2,0:T(8,128)(2,1)S(1)} %pad_maximum_fusion.19), channel_id=1, source_target_pairs={{0,6},{2,4},{4,2},{6,0},{1,7},{3,5},{5,3},{7,1},{8,14},{10,12},{12... | collective-permute-start | bytes 3145736 | tf_op jit(solution)/shard_map/ppermute | solution.py:115
  295.7 46.9 %collective-permute-start.46 = (bf16[4,128,1024]{1,2,0:T(8,128)(2,1)S(1)}, bf16[4,128,1024]{1,2,0:T(8,128)(2,1)S(1)}, u32[]{:S(2)}, u32[]{:S(2)}) collective-permute-start(bf16[4,128,1024]{1,2,0:T(8,128)(2,1)S(1)} %pad_maximum_fusion.18), channel_id=1, source_target_pairs={{0,4},{2,6},{4,0},{6,2},{1,5},{3,7},{5,1},{7,3},{8,12},{10,14},{12... | collective-permute-start | bytes 3145736 | tf_op jit(solution)/shard_map/ppermute | solution.py:115
  296.4 46.2 %collective-permute-start.45 = (bf16[4,128,1024]{1,2,0:T(8,128)(2,1)S(1)}, bf16[4,128,1024]{1,2,0:T(8,128)(2,1)S(1)}, u32[]{:S(2)}, u32[]{:S(2)}) collective-permute-start(bf16[4,128,1024]{1,2,0:T(8,128)(2,1)S(1)} %pad_maximum_fusion.17), channel_id=1, source_target_pairs={{0,2},{2,0},{4,6},{6,4},{1,3},{3,1},{5,7},{7,5},{8,10},{10,8},{12,... | collective-permute-start | bytes 3145736 | tf_op jit(solution)/shard_map/ppermute | solution.py:115
  344.2 196.9 %reduce-scatter.8.cloned.1.call-start = ((), (), s32[]{:S(2)}) async-start(), calls=%async_computation.7 | async-start | bytes 5013504 | tf_op jit(solution)/shard_map/reduce_scatter | solution.py:259
  385.1 143.7 %collective-permute-start.38 = (bf16[2048,256]{1,0:T(8,128)(2,1)}, bf16[2048,256]{1,0:T(8,128)(2,1)}, u32[]{:S(2)}, u32[]{:S(2)}) collective-permute-start(bf16[2048,256]{1,0:T(8,128)(2,1)} %convolution_convert_fusion.3), channel_id=1, source_target_pairs={{0,2},{2,0},{4,6},{6,4},{1,3},{3,1},{5,7},{7,5},{8,10},{10,8},{12,... | collective-permute-start | bytes 3145736 | tf_op jit(solution)/shard_map/ppermute | solution.py:115
  407.5 123.5 %collective-permute-start.39 = (bf16[2048,256]{1,0:T(8,128)(2,1)}, bf16[2048,256]{1,0:T(8,128)(2,1)}, u32[]{:S(2)}, u32[]{:S(2)}) collective-permute-start(bf16[2048,256]{1,0:T(8,128)(2,1)} %convolution_convert_fusion.2), channel_id=1, source_target_pairs={{0,4},{2,6},{4,0},{6,2},{1,5},{3,7},{5,1},{7,3},{8,12},{10,14},{12... | collective-permute-start | bytes 3145736 | tf_op jit(solution)/shard_map/ppermute | solution.py:115
  422.3 111.0 %collective-permute-start.40 = (bf16[2048,256]{1,0:T(8,128)(2,1)}, bf16[2048,256]{1,0:T(8,128)(2,1)}, u32[]{:S(2)}, u32[]{:S(2)}) collective-permute-start(bf16[2048,256]{1,0:T(8,128)(2,1)} %convolution_convert_fusion.1), channel_id=1, source_target_pairs={{0,6},{2,4},{4,2},{6,0},{1,7},{3,5},{5,3},{7,1},{8,14},{10,12},{12... | collective-permute-start | bytes 3145736 | tf_op jit(solution)/shard_map/ppermute | solution.py:115
  431.4 86.6 %collective-permute-start.35 = (bf16[128,1024]{1,0:T(8,128)(2,1)S(1)}, bf16[128,1024]{1,0:T(8,128)(2,1)S(1)}, u32[]{:S(2)}, u32[]{:S(2)}) collective-permute-start(bf16[128,1024]{1,0:T(8,128)(2,1)S(1)} %get-tuple-element.111), channel_id=1, source_target_pairs={{0,2},{2,0},{4,6},{6,4},{1,3},{3,1},{5,7},{7,5},{8,10},{10,8},{12,... | collective-permute-start | bytes 786440 | tf_op jit(solution)/shard_map/ppermute | solution.py:115
  432.1 86.6 %collective-permute-start.36 = (bf16[128,1024]{1,0:T(8,128)(2,1)S(1)}, bf16[128,1024]{1,0:T(8,128)(2,1)S(1)}, u32[]{:S(2)}, u32[]{:S(2)}) collective-permute-start(bf16[128,1024]{1,0:T(8,128)(2,1)S(1)} %get-tuple-element.111), channel_id=1, source_target_pairs={{0,4},{2,6},{4,0},{6,2},{1,5},{3,7},{5,1},{7,3},{8,12},{10,14},{12... | collective-permute-start | bytes 786440 | tf_op jit(solution)/shard_map/ppermute | solution.py:115
  (136 other events, 1481.5 us)
Sparse Core Ops, SparseCore 0:
  11.9 30.7 all-gather.10
  44.8 21.2 all-gather.6
  68.2 48.8 all-gather.8
  287.4 31.6 reduce-scatter.3
  344.3 26.2 reduce-scatter.5
  372.8 50.8 reduce-scatter.7
